TPU v7x, 128 devices: a whole 4x4x4 slice. The times are simulated.
128 devices in a mesh: member: 16 (over z_lo, y, core), band: 8 (over x, z_hi).
Axes of the slice: x: 4, y: 4, z: 4 (z_hi: 2, z_lo: 2; z = z_hi * 2 + z_lo), core: 2. Of those that a mesh axis runs over, the one named last changes fastest.
Arguments:
- height_start: float32 [80, 512, 1024], P(None, 'member', 'band'), may hold values from -6 to 6
- east_start: float32 [80, 512, 1024], P(None, 'member', 'band'), may hold values from -6 to 6
- north_start: float32 [80, 512, 1024], P(None, 'member', 'band'), may hold values from -6 to 6
- obs_value: float32 [512, 1024], P('member', 'band'), may hold values from -8 to 8
- obs_mask: int32 [512, 1024], P('member', 'band'), may hold values 0 or 1
- obs_precision: float32 [512, 1024], P('member', 'band'), may hold values from 0.25 to 4
- step_sizes: int32 [2], replicated, may hold values from 4 to 12
Outputs:
- analysis_height: float32 [80, 512, 1024], P(None, 'member', 'band')
- analysis_east: float32 [80, 512, 1024], P(None, 'member', 'band')
- analysis_north: float32 [80, 512, 1024], P(None, 'member', 'band')
All inputs are finite; a program needn't handle non-finite values. No bound on the sum of `obs_mask` on one device may be relied on, other than what follows from the above.
Results may differ from a plain program's by a relative error of at most 0.0001.
Values sent between devices are 32-bit elements; how exact they have to be, the bound alone decides.
A program may use at most 128 MiB of HBM per device.

v0:
```python
import jax
import jax.numpy as jnp
from jax import lax
from jax.sharding import Mesh
from jax.sharding import PartitionSpec as P

STEPS = 3
ITERS = 2
LWIDTH = 32
LSCALE = 12
MEMBER = ("member_0", "member_1", "member_2")
BAND = ("band_0", "band_1")
MEMBER_BAND = ("member_0", "member_1", "member_2", "band_0", "band_1")
highest = lax.Precision.HIGHEST


def extended(block, sides, width, periodic):
    for axis, dim in sides:
        count = lax.axis_size(axis)
        forward = [(i, i + 1) for i in range(count - 1)]
        if periodic:
            forward.append((count - 1, 0))
        backward = [(target, source) for source, target in forward]
        low = lax.ppermute(
            lax.slice_in_dim(block, block.shape[dim] - width, None, axis=dim), axis, forward
        )
        high = lax.ppermute(lax.slice_in_dim(block, 0, width, axis=dim), axis, backward)
        block = jnp.concatenate([low, block, high], axis=dim)
    return block


def one_axis_at_a_time(array, axes):
    for axis in axes:
        array = lax.psum(array, axis)
    return array


def taper_kernel(outputs, inputs, margin, spread):
    out_index = jnp.arange(outputs, dtype=jnp.int32)[:, None]
    in_index = jnp.arange(inputs, dtype=jnp.int32)[None, :]
    offset = (in_index - margin - out_index).astype(jnp.float32)
    scaled_off = offset / spread
    weight = jnp.exp(-0.5 * scaled_off * scaled_off)
    return jnp.where(jnp.abs(offset) <= margin, weight, jnp.zeros_like(weight))


def taper_rows(padded, row_count, margin, spread):
    kernel = taper_kernel(row_count, row_count + 2 * margin, margin, spread)
    return jnp.einsum("ab,mbc->mac", kernel, padded, precision=highest)


def taper_columns(padded, columns, margin, spread):
    block_size = 128
    windows = jnp.stack([padded], axis=2)
    kernel = taper_kernel(block_size, block_size + 2 * margin, margin, spread)
    result = jnp.einsum("mrjk,bk->mrjb", windows, kernel, precision=highest)
    return result.reshape(padded.shape[0], padded.shape[1], columns)


def wave_edges(stacked, margin):
    rows_done = extended(stacked, ((MEMBER, 2),), margin, False)
    return extended(rows_done, ((BAND, 3),), margin, True)


def advance_deep(height, eastward, northward, valid_rows):
    padded = wave_edges(jnp.stack([height, eastward, northward]), 2)
    height_pad = padded[0]
    east_pad = padded[1]
    north_pad = padded[2]
    wide_height = height_pad[:, 1:-1, 1:-1] - 0.2 * (
        east_pad[:, 1:-1, 2:]
        - east_pad[:, 1:-1, :-2]
        + (north_pad[:, 2:, 1:-1] - north_pad[:, :-2, 1:-1])
    )
    wide_height = jnp.where(valid_rows[None, :, None], wide_height, jnp.zeros_like(wide_height))
    new_height = wide_height[:, 1:-1, 1:-1]
    new_east = (
        eastward + 0.1 * northward - 0.2 * (wide_height[:, 1:-1, 2:] - wide_height[:, 1:-1, :-2])
    )
    new_north = (
        northward - 0.1 * eastward - 0.2 * (wide_height[:, 2:, 1:-1] - wide_height[:, :-2, 1:-1])
    )
    return (new_height, new_east, new_north)


def descend(anomalies, member_means, observed, step_sizes, cell_total, gather_state, localize):
    weights = jnp.zeros_like(anomalies[0])
    for iteration in range(ITERS):
        if iteration == 0:
            analysis_state = member_means
        else:
            analysis_state = member_means + gather_state(jnp.sum(anomalies * weights[None], axis=1))
        residual = observed[1] * (
            observed[0]
            - analysis_state[0]
            - 0.15 * (analysis_state[1] * analysis_state[1] + analysis_state[2] * analysis_state[2])
        )
        contrib = (
            anomalies[0]
            + 0.3 * (analysis_state[1] * anomalies[1] + analysis_state[2] * anomalies[2])
        ) * residual
        gradient = weights - localize(contrib)
        square_total = one_axis_at_a_time(jnp.sum(gradient * gradient), MEMBER_BAND)
        factor = (
            step_sizes[iteration].astype(jnp.float32)
            / 64.0
            / jnp.sqrt(square_total / cell_total + 1e-06)
        )
        weights = weights - factor * gradient
    return weights


def analyse_tiles(ensemble, observed, step_sizes, cell_total, root_scale, members):
    member_means = jnp.sum(ensemble, axis=1) / members
    anomalies = (ensemble - member_means[:, None]) / root_scale

    def local_state(partial_sum):
        return partial_sum

    def localize(contrib):
        padded = extended(contrib, ((MEMBER, 1),), LWIDTH, False)
        lat_done = taper_rows(padded, contrib.shape[1], LWIDTH, LSCALE)
        wrapped = extended(lat_done, ((BAND, 2),), LWIDTH, True)
        return taper_columns(wrapped, contrib.shape[2], LWIDTH, LSCALE)

    weights = descend(
        anomalies, member_means, observed, step_sizes, cell_total, local_state, localize
    )
    return jnp.sum(anomalies * weights[None], axis=1)


def per_device(
    height_start, east_start, north_start, obs_value, obs_mask, obs_precision, step_sizes
):
    members = height_start.shape[0]
    row_count = height_start.shape[1]
    col_count = height_start.shape[2]
    height, eastward, northward = (height_start, east_start, north_start)
    global_rows = (
        lax.axis_index(MEMBER) * row_count - 1 + jnp.arange(row_count + 2, dtype=jnp.int32)
    )
    valid_rows = (global_rows >= 0) & (global_rows < row_count * lax.axis_size(MEMBER))
    for section_number in range(STEPS):
        height, eastward, northward = advance_deep(height, eastward, northward, valid_rows)
    ensemble = jnp.stack([height, eastward, northward])
    obs_weight = obs_mask.astype(jnp.float32) * obs_precision
    observed = jnp.stack([obs_value, obs_weight])
    cell_total = float(
        members * row_count * col_count * lax.axis_size(MEMBER) * lax.axis_size(BAND)
    )
    root_scale = jnp.sqrt(jnp.float32(members - 1))
    increment = analyse_tiles(ensemble, observed, step_sizes, cell_total, root_scale, members)
    analysis = ensemble + increment[:, None]
    return (analysis[0], analysis[1], analysis[2])


def solution(mesh):
    torus = Mesh(
        mesh.devices.reshape(2, 4, 2, 4, 2),
        ("member_0", "member_1", "member_2", "band_0", "band_1"),
    )
    in_specs = (
        P(None, MEMBER, BAND),
        P(None, MEMBER, BAND),
        P(None, MEMBER, BAND),
        P(MEMBER, BAND),
        P(MEMBER, BAND),
        P(MEMBER, BAND),
        P(),
    )
    out_specs = (P(None, MEMBER, BAND), P(None, MEMBER, BAND), P(None, MEMBER, BAND))
    return jax.shard_map(
        per_device, mesh=torus, in_specs=in_specs, out_specs=out_specs, check_vma=False
    )
```

profile of v0, /device:TPU:2, one launch (start us, length us, event | category | flops | bytes accessed | tf_op | source)
XLA Modules:
  0.0 401.4 jit_solution(12849979625109068279)
XLA Ops:
  0.7 2.5 pad_maximum_fusion.15
  6.2 3.4 collective-permute-done.1
  9.7 2.1 pad_maximum_fusion.3
  11.8 5.3 %fusion.117 = (f32[3,80,36,2]{3,2,1,0:T(8,128)}, f32[3,80,36,2]{3,2,1,0:T(8,128)}) fusion(f32[3,80,36,128]{3,2,1,0:T(8,128)S(1)} %pad_maximum_fusion.3), kind=kLoop, calls=%fused_computation.180 | loop fusion | bytes 276480 | tf_op jit(solution)/shard_map/slice | solution.py:25
  17.1 3.8 copy.10
  20.9 3.9 collective-permute-start.2
  24.9 3.8 copy.11
  30.4 3.6 copy.12
  35.5 3.5 copy.13
  39.0 10.7 %pad_maximum_fusion = f32[3,80,36,132]{3,2,1,0:T(8,128)S(1)} fusion(f32[3,80,36,2]{3,2,1,0:T(8,128)} %copy.13, f32[3,80,2,128]{3,2,1,0:T(2,128)S(1)} %collective-permute-done.1, f32[1,80,32,128]{3,2,1,0:T(8,128)S(1)} %bitcast.125, f32[1,80,32,128]{3,2,1,0:T(8,128)S(1)} %bitcast.128, f32[1,80,32,128]{3,2,1,0:T(8,128)} %bitcast.131, ...), kind=kLoop, calls=%fused_computation | loop fusion | flops 6842880 | bytes 9123840 | tf_op jit(solution)/shard_map/concatenate | solution.py:28
  49.7 2.3 slice_bitcast_fusion.8
  52.0 5.8 %fusion.23 = f32[80,34,130]{2,1,0:T(8,128)S(1)} fusion(f32[80,36,132]{2,1,0:T(8,128)S(1)} %get-tuple-element.10, f32[80,36,132]{2,1,0:T(8,128)S(1)} %get-tuple-element.11, f32[80,36,132]{2,1,0:T(8,128)} %get-tuple-element.9, pred[34]{0:T(512)(128)(4,1)S(1)} %copy-done.24), kind=kLoop, calls=%fused_computation.44 | loop fusion | flops 2121600 | bytes 8486434 | tf_op jit(solution)/shard_map/jit(_where)/select_n | solution.py:75
  59.5 5.1 %collective-permute-start.4 = (f32[3,80,2,128]{3,2,1,0:T(2,128)S(1)}, f32[3,80,2,128]{3,2,1,0:T(2,128)S(1)}, u32[]{:S(2)}, u32[]{:S(2)}) collective-permute-start(f32[3,80,2,128]{3,2,1,0:T(2,128)S(1)} %get-tuple-element.29), channel_id=1, source_target_pairs={{0,8},{8,16},{16,24},{24,32},{32,40},{40,48},{48,56},{56,64},{64,7... | collective-permute-start | bytes 737288 | tf_op jit(solution)/shard_map/ppermute | solution.py:24
  66.1 3.3 collective-permute-done.5
  70.4 5.3 %fusion.116 = (f32[3,80,36,2]{3,2,1,0:T(8,128)}, f32[3,80,36,2]{3,2,1,0:T(8,128)}) fusion(f32[3,80,36,128]{3,2,1,0:T(8,128)S(1)} %pad_maximum_fusion.4), kind=kLoop, calls=%fused_computation.179 | loop fusion | bytes 276480 | tf_op jit(solution)/shard_map/slice | solution.py:25
  75.7 3.8 copy.14
  81.1 3.8 copy.15
  84.9 3.0 collective-permute-start.7
  87.9 3.6 copy.16
  91.6 3.5 copy.17
  95.1 10.7 %pad_maximum_fusion.1 = f32[3,80,36,132]{3,2,1,0:T(8,128)S(1)} fusion(f32[3,80,36,2]{3,2,1,0:T(8,128)} %copy.17, f32[3,80,2,128]{3,2,1,0:T(2,128)S(1)} %collective-permute-done.5, f32[1,80,32,128]{3,2,1,0:T(8,128)S(1)} %bitcast.122, f32[1,80,32,128]{3,2,1,0:T(8,128)S(1)} %bitcast.119, f32[1,80,32,128]{3,2,1,0:T(8,128)} %copy-done.18, ...), kind=kLoop, calls=%fused_computation.1 | loop fusion | flops 6842880 | bytes 9123840 | tf_op jit(solution)/shard_map/concatenate | solution.py:28
  105.8 2.3 slice_bitcast_fusion.5
  108.1 5.8 %fusion.19 = f32[80,34,130]{2,1,0:T(8,128)S(1)} fusion(f32[80,36,132]{2,1,0:T(8,128)S(1)} %get-tuple-element.7, f32[80,36,132]{2,1,0:T(8,128)S(1)} %get-tuple-element.8, f32[80,36,132]{2,1,0:T(8,128)} %get-tuple-element.6, pred[34]{0:T(512)(128)(4,1)S(1)} %copy-done.25), kind=kLoop, calls=%fused_computation.35 | loop fusion | flops 2121600 | bytes 8486434 | tf_op jit(solution)/shard_map/jit(_where)/select_n | solution.py:75
  115.6 5.9 %collective-permute-start.8 = (f32[3,80,2,128]{3,2,1,0:T(2,128)S(1)}, f32[3,80,2,128]{3,2,1,0:T(2,128)S(1)}, u32[]{:S(2)}, u32[]{:S(2)}) collective-permute-start(f32[3,80,2,128]{3,2,1,0:T(2,128)S(1)} %get-tuple-element.27), channel_id=1, source_target_pairs={{0,8},{8,16},{16,24},{24,32},{32,40},{40,48},{48,56},{56,64},{64,7... | collective-permute-start | bytes 737288 | tf_op jit(solution)/shard_map/ppermute | solution.py:24
  125.9 5.3 %fusion.115 = (f32[3,80,36,2]{3,2,1,0:T(8,128)}, f32[3,80,36,2]{3,2,1,0:T(8,128)}) fusion(f32[3,80,36,128]{3,2,1,0:T(8,128)S(1)} %pad_maximum_fusion.5), kind=kLoop, calls=%fused_computation.178 | loop fusion | bytes 276480 | tf_op jit(solution)/shard_map/slice | solution.py:25
  131.2 3.8 copy.18
  135.1 3.9 collective-permute-start.10
  139.0 3.8 copy.19
  143.5 3.6 copy.20
  147.0 2.1 collective-permute-done.11
  149.1 3.5 copy.21
  152.6 10.7 %pad_maximum_fusion.2 = f32[3,80,36,132]{3,2,1,0:T(8,128)S(1)} fusion(f32[3,80,36,2]{3,2,1,0:T(8,128)} %copy.21, f32[3,80,2,128]{3,2,1,0:T(2,128)S(1)} %collective-permute-done.9, f32[1,80,32,128]{3,2,1,0:T(8,128)S(1)} %bitcast.116, f32[1,80,32,128]{3,2,1,0:T(8,128)S(1)} %bitcast.113, f32[1,80,32,128]{3,2,1,0:T(8,128)} %copy-done.17, ...), kind=kLoop, calls=%fused_computation.2 | loop fusion | flops 6842880 | bytes 9123840 | tf_op jit(solution)/shard_map/concatenate | solution.py:28
  163.4 2.3 slice_bitcast_fusion.2
  165.7 5.6 %fusion.15 = f32[80,34,130]{2,1,0:T(8,128)S(1)} fusion(f32[80,36,132]{2,1,0:T(8,128)S(1)} %get-tuple-element.4, f32[80,36,132]{2,1,0:T(8,128)S(1)} %get-tuple-element.5, f32[80,36,132]{2,1,0:T(8,128)} %get-tuple-element.3, pred[34]{0:T(512)(128)(4,1)S(1)} %copy-done.26), kind=kLoop, calls=%fused_computation.26 | loop fusion | flops 2121600 | bytes 8486434 | tf_op jit(solution)/shard_map/jit(_where)/select_n | solution.py:75
  175.8 5.2 %collective-permute-start.12 = (f32[80,32,128]{2,1,0:T(8,128)S(1)}, f32[80,32,128]{2,1,0:T(8,128)S(1)}, u32[]{:S(2)}, u32[]{:S(2)}) collective-permute-start(f32[80,32,128]{2,1,0:T(8,128)S(1)} %add_multiply_fusion.1), channel_id=1, source_target_pairs={{0,8},{8,16},{16,24},{24,32},{32,40},{40,48},{48,56},{56,64},{64,7... | collective-permute-start | bytes 3932168 | tf_op jit(solution)/shard_map/ppermute | solution.py:24
  183.5 3.1 collective-permute-done.13
  186.6 2.3 fusion.39
  195.4 2.8 copy.23
  198.2 3.0 collective-permute-start.15
  201.2 23.3 %collective-permute-done.14 = f32[80,32,32]{0,2,1:T(8,128)} collective-permute-done((f32[80,32,32]{0,2,1:T(8,128)S(1)}, f32[80,32,32]{0,2,1:T(8,128)}, u32[]{:S(2)}, u32[]{:S(2)}) %collective-permute-start.14) | collective-permute-done | bytes 327712 | tf_op jit(solution)/shard_map/ppermute | solution.py:24
  224.5 3.0 copy.24
  227.6 3.0 copy.25
  230.6 6.4 %multiply_reduce_fusion.3 = (f32[]{:T(128)}, f32[80,32,128]{2,1,0:T(8,128)}) fusion(s32[192]{0:T(256)S(1)} %iota_add_fusion, f32[80,32,32]{2,1,0:T(8,128)} %copy.25, f32[80,32,128]{2,1,0:T(8,128)} %copy-done.20, f32[80,32,32]{2,1,0:T(8,128)} %copy.24), kind=kOutput, calls=%fused_computation.99 | convolution fusion | flops 757137408 | bytes 3277572 | tf_op jit(solution)/shard_map/mrjk,bk->mrjb/dot_general | solution.py:56
  237.1 14.6 %psum.70 = f32[]{:T(128)} all-reduce(f32[]{:T(128)} %get-tuple-element.46), channel_id=1, replica_groups=mesh['member_0'=2,'member_1'=4,'member_2'=2,'band_0'=4,'band_1'=2] {'mem..., use_global_device_ids=true, to_apply=%region_2.3 | all-reduce | flops 1 | bytes 8 | tf_op jit(solution)/shard_map/psum | solution.py:34
  251.6 9.2 %psum.71 = f32[]{:T(128)} all-reduce(f32[]{:T(128)} %psum.70), channel_id=1, replica_groups=mesh['member_0'=2,'member_1'=4,'member_2'=2,'band_0'=4,'band_1'=2] {'mem..., use_global_device_ids=true, to_apply=%region_3.4 | all-reduce | flops 1 | bytes 8 | tf_op jit(solution)/shard_map/psum | solution.py:34
  261.4 5.0 %psum.72 = f32[]{:T(128)} all-reduce(f32[]{:T(128)} %psum.71), channel_id=1, replica_groups=mesh['member_0'=2,'member_1'=4,'member_2'=2,'band_0'=4,'band_1'=2] {'mem..., use_global_device_ids=true, to_apply=%region_4.5 | all-reduce | flops 1 | bytes 8 | tf_op jit(solution)/shard_map/psum | solution.py:34
  267.1 10.8 %psum.73 = f32[]{:T(128)} all-reduce(f32[]{:T(128)} %psum.72), channel_id=1, replica_groups=mesh['member_0'=2,'member_1'=4,'member_2'=2,'band_0'=4,'band_1'=2] {'ban..., use_global_device_ids=true, to_apply=%region_5.6 | all-reduce | flops 1 | bytes 8 | tf_op jit(solution)/shard_map/psum | solution.py:34
  277.9 7.2 %psum.74 = f32[]{:T(128)} all-reduce(f32[]{:T(128)} %psum.73), channel_id=1, replica_groups=mesh['member_0'=2,'member_1'=4,'member_2'=2,'band_0'=4,'band_1'=2] {'ban..., use_global_device_ids=true, to_apply=%region_6.7 | all-reduce | flops 1 | bytes 8 | tf_op jit(solution)/shard_map/psum | solution.py:34
  294.0 2.7 collective-permute-done.17
  296.7 2.3 fusion.36
  304.0 3.6 collective-permute-start.18
  307.6 2.8 copy.27
  310.4 2.7 collective-permute-start.19
  313.1 7.0 %collective-permute-done.18 = f32[80,32,32]{0,2,1:T(8,128)} collective-permute-done((f32[80,32,32]{0,2,1:T(8,128)S(1)}, f32[80,32,32]{0,2,1:T(8,128)}, u32[]{:S(2)}, u32[]{:S(2)}) %collective-permute-start.18) | collective-permute-done | bytes 327712 | tf_op jit(solution)/shard_map/ppermute | solution.py:24
  320.0 3.0 copy.28
  324.2 3.0 copy.29
  327.2 6.8 %multiply_reduce_fusion.2 = (f32[]{:T(128)}, f32[80,32,128]{2,1,0:T(8,128)}) fusion(s32[192]{0:T(256)S(1)} %iota_add_fusion, f32[80,32,32]{2,1,0:T(8,128)} %copy.29, f32[80,32,128]{2,1,0:T(8,128)} %copy-done.19, f32[80,32,32]{2,1,0:T(8,128)} %copy.28, f32[80,32,128]{2,1,0:T(8,128)} %get-tuple-element.47, f32[]{:T(128)S(6)} %div.55), kind=kOutput, calls=%fused_computation.96 | convolution fusion | flops 757792768 | bytes 4588296 | tf_op jit(solution)/shard_map/mrjk,bk->mrjb/dot_general | solution.py:56
  334.0 28.9 %psum.75 = f32[]{:T(128)} all-reduce(f32[]{:T(128)} %get-tuple-element.48), channel_id=1, replica_groups=mesh['member_0'=2,'member_1'=4,'member_2'=2,'band_0'=4,'band_1'=2] {'mem..., use_global_device_ids=true, to_apply=%region_9.10 | all-reduce | flops 1 | bytes 8 | tf_op jit(solution)/shard_map/psum | solution.py:34
  363.0 9.3 %psum.76 = f32[]{:T(128)} all-reduce(f32[]{:T(128)} %psum.75), channel_id=1, replica_groups=mesh['member_0'=2,'member_1'=4,'member_2'=2,'band_0'=4,'band_1'=2] {'mem..., use_global_device_ids=true, to_apply=%region_10.11 | all-reduce | flops 1 | bytes 8 | tf_op jit(solution)/shard_map/psum | solution.py:34
  372.3 3.1 psum.77
  376.1 11.4 %psum.78 = f32[]{:T(128)} all-reduce(f32[]{:T(128)} %psum.77), channel_id=1, replica_groups=mesh['member_0'=2,'member_1'=4,'member_2'=2,'band_0'=4,'band_1'=2] {'ban..., use_global_device_ids=true, to_apply=%region_12.13 | all-reduce | flops 1 | bytes 8 | tf_op jit(solution)/shard_map/psum | solution.py:34
  387.4 7.6 %psum.79 = f32[]{:T(128)} all-reduce(f32[]{:T(128)} %psum.78), channel_id=1, replica_groups=mesh['member_0'=2,'member_1'=4,'member_2'=2,'band_0'=4,'band_1'=2] {'ban..., use_global_device_ids=true, to_apply=%region_13.14 | all-reduce | flops 1 | bytes 8 | tf_op jit(solution)/shard_map/psum | solution.py:34
  395.7 2.1 subtract_multiply_fusion.1
  399.2 2.0 slice_bitcast_fusion.9
  (109 shorter events, 48.0 us)
Async XLA Ops:
  0.6 9.0 %copy-start.15 = (f32[80,32,128]{2,1,0:T(8,128)S(1)}, f32[80,32,128]{2,1,0:T(8,128)}, u32[]{:S(2)}) copy-start(f32[80,32,128]{2,1,0:T(8,128)} %param.8) | copy-start | bytes 3932164
  0.6 9.0 %copy-start.13 = (f32[80,32,128]{2,1,0:T(8,128)S(1)}, f32[80,32,128]{2,1,0:T(8,128)}, u32[]{:S(2)}) copy-start(f32[80,32,128]{2,1,0:T(8,128)} %param.9) | copy-start | bytes 3932164
  3.2 3.1 collective-permute-start
  4.9 4.8 %collective-permute-start.1 = (f32[3,80,2,128]{3,2,1,0:T(2,128)S(1)}, f32[3,80,2,128]{3,2,1,0:T(2,128)S(1)}, u32[]{:S(2)}, u32[]{:S(2)}) collective-permute-start(f32[3,80,2,128]{3,2,1,0:T(2,128)S(1)} %get-tuple-element.32), channel_id=1, source_target_pairs={{8,0},{16,8},{24,16},{32,24},{40,32},{48,40},{56,48},{64,56},{72,6... | collective-permute-start | bytes 737288 | tf_op jit(solution)/shard_map/ppermute | solution.py:27
  20.9 9.5 %collective-permute-start.2 = (f32[3,80,36,2]{1,3,2,0:T(2,128)S(1)}, f32[3,80,36,2]{1,3,2,0:T(2,128)S(1)}, u32[]{:S(2)}, u32[]{:S(2)}) collective-permute-start(f32[3,80,36,2]{1,3,2,0:T(2,128)S(1)} %copy.10), channel_id=1, source_target_pairs={{0,1},{1,2},{2,3},{3,4},{4,5},{5,6},{6,7},{7,0},{8,9},{9,10},{10,1... | collective-permute-start | bytes 207368 | tf_op jit(solution)/shard_map/ppermute | solution.py:24
  28.7 6.8 %collective-permute-start.3 = (f32[3,80,36,2]{1,3,2,0:T(2,128)S(1)}, f32[3,80,36,2]{1,3,2,0:T(2,128)S(1)}, u32[]{:S(2)}, u32[]{:S(2)}) collective-permute-start(f32[3,80,36,2]{1,3,2,0:T(2,128)S(1)} %copy.11), channel_id=1, source_target_pairs={{1,0},{2,1},{3,2},{4,3},{5,4},{6,5},{7,6},{0,7},{9,8},{10,9},{11,1... | collective-permute-start | bytes 207368 | tf_op jit(solution)/shard_map/ppermute | solution.py:27
  49.7 2.3 copy-start.24
  52.0 5.9 %copy-start.14 = (f32[80,32,128]{2,1,0:T(8,128)S(1)}, f32[80,32,128]{2,1,0:T(8,128)}, u32[]{:S(2)}) copy-start(f32[80,32,128]{2,1,0:T(8,128)} %param.9) | copy-start | bytes 3932164
  52.0 5.9 %copy-start.16 = (f32[80,32,128]{2,1,0:T(8,128)S(1)}, f32[80,32,128]{2,1,0:T(8,128)}, u32[]{:S(2)}) copy-start(f32[80,32,128]{2,1,0:T(8,128)} %param.8) | copy-start | bytes 3932164
  59.3 16.4 %copy-start.18 = (f32[1,80,32,128]{3,2,1,0:T(8,128)}, f32[1,80,32,128]{3,2,1,0:T(8,128)S(1)}, u32[]{:S(2)}) copy-start(f32[1,80,32,128]{3,2,1,0:T(8,128)S(1)} %get-tuple-element.35) | copy-start | bytes 3932164
  59.3 35.7 %copy-start.9 = (f32[80,32,128]{2,1,0:T(8,128)}, f32[80,32,128]{2,1,0:T(8,128)S(1)}, u32[]{:S(2)}) copy-start(f32[80,32,128]{2,1,0:T(8,128)S(1)} %get-tuple-element.16) | copy-start | bytes 3932164
  59.3 35.7 %copy-start.11 = (f32[80,32,128]{2,1,0:T(8,128)}, f32[80,32,128]{2,1,0:T(8,128)S(1)}, u32[]{:S(2)}) copy-start(f32[80,32,128]{2,1,0:T(8,128)S(1)} %get-tuple-element.17) | copy-start | bytes 3932164
  59.5 6.6 %collective-permute-start.4 = (f32[3,80,2,128]{3,2,1,0:T(2,128)S(1)}, f32[3,80,2,128]{3,2,1,0:T(2,128)S(1)}, u32[]{:S(2)}, u32[]{:S(2)}) collective-permute-start(f32[3,80,2,128]{3,2,1,0:T(2,128)S(1)} %get-tuple-element.29), channel_id=1, source_target_pairs={{0,8},{8,16},{16,24},{24,32},{32,40},{40,48},{48,56},{56,64},{64,7... | collective-permute-start | bytes 737288 | tf_op jit(solution)/shard_map/ppermute | solution.py:24
  64.6 4.8 %collective-permute-start.5 = (f32[3,80,2,128]{3,2,1,0:T(2,128)S(1)}, f32[3,80,2,128]{3,2,1,0:T(2,128)S(1)}, u32[]{:S(2)}, u32[]{:S(2)}) collective-permute-start(f32[3,80,2,128]{3,2,1,0:T(2,128)S(1)} %get-tuple-element.30), channel_id=1, source_target_pairs={{8,0},{16,8},{24,16},{32,24},{40,32},{48,40},{56,48},{64,56},{72,6... | collective-permute-start | bytes 737288 | tf_op jit(solution)/shard_map/ppermute | solution.py:27
  79.5 8.4 %collective-permute-start.6 = (f32[3,80,36,2]{1,3,2,0:T(2,128)S(1)}, f32[3,80,36,2]{1,3,2,0:T(2,128)S(1)}, u32[]{:S(2)}, u32[]{:S(2)}) collective-permute-start(f32[3,80,36,2]{1,3,2,0:T(2,128)S(1)} %copy.14), channel_id=1, source_target_pairs={{0,1},{1,2},{2,3},{3,4},{4,5},{5,6},{6,7},{7,0},{8,9},{9,10},{10,1... | collective-permute-start | bytes 207368 | tf_op jit(solution)/shard_map/ppermute | solution.py:24
  84.9 6.7 %collective-permute-start.7 = (f32[3,80,36,2]{1,3,2,0:T(2,128)S(1)}, f32[3,80,36,2]{1,3,2,0:T(2,128)S(1)}, u32[]{:S(2)}, u32[]{:S(2)}) collective-permute-start(f32[3,80,36,2]{1,3,2,0:T(2,128)S(1)} %copy.15), channel_id=1, source_target_pairs={{1,0},{2,1},{3,2},{4,3},{5,4},{6,5},{7,6},{0,7},{9,8},{10,9},{11,1... | collective-permute-start | bytes 207368 | tf_op jit(solution)/shard_map/ppermute | solution.py:27
  105.8 2.3 copy-start.25
  108.1 5.9 %copy-start.10 = (f32[80,32,128]{2,1,0:T(8,128)S(1)}, f32[80,32,128]{2,1,0:T(8,128)}, u32[]{:S(2)}) copy-start(f32[80,32,128]{2,1,0:T(8,128)} %copy-done.9) | copy-start | bytes 3932164
  108.1 5.9 %copy-start.12 = (f32[80,32,128]{2,1,0:T(8,128)S(1)}, f32[80,32,128]{2,1,0:T(8,128)}, u32[]{:S(2)}) copy-start(f32[80,32,128]{2,1,0:T(8,128)} %copy-done.11) | copy-start | bytes 3932164
  115.4 15.8 %copy-start.17 = (f32[1,80,32,128]{3,2,1,0:T(8,128)}, f32[1,80,32,128]{3,2,1,0:T(8,128)S(1)}, u32[]{:S(2)}) copy-start(f32[1,80,32,128]{3,2,1,0:T(8,128)S(1)} %get-tuple-element.34) | copy-start | bytes 3932164
  115.4 37.2 %copy-start.5 = (f32[80,32,128]{2,1,0:T(8,128)}, f32[80,32,128]{2,1,0:T(8,128)S(1)}, u32[]{:S(2)}) copy-start(f32[80,32,128]{2,1,0:T(8,128)S(1)} %get-tuple-element.14) | copy-start | bytes 3932164
  115.4 37.2 %copy-start.7 = (f32[80,32,128]{2,1,0:T(8,128)}, f32[80,32,128]{2,1,0:T(8,128)S(1)}, u32[]{:S(2)}) copy-start(f32[80,32,128]{2,1,0:T(8,128)S(1)} %get-tuple-element.15) | copy-start | bytes 3932164
  115.6 7.6 %collective-permute-start.8 = (f32[3,80,2,128]{3,2,1,0:T(2,128)S(1)}, f32[3,80,2,128]{3,2,1,0:T(2,128)S(1)}, u32[]{:S(2)}, u32[]{:S(2)}) collective-permute-start(f32[3,80,2,128]{3,2,1,0:T(2,128)S(1)} %get-tuple-element.27), channel_id=1, source_target_pairs={{0,8},{8,16},{16,24},{24,32},{32,40},{40,48},{48,56},{56,64},{64,7... | collective-permute-start | bytes 737288 | tf_op jit(solution)/shard_map/ppermute | solution.py:24
  121.6 3.4 collective-permute-start.9
  135.1 8.4 %collective-permute-start.10 = (f32[3,80,36,2]{1,3,2,0:T(2,128)S(1)}, f32[3,80,36,2]{1,3,2,0:T(2,128)S(1)}, u32[]{:S(2)}, u32[]{:S(2)}) collective-permute-start(f32[3,80,36,2]{1,3,2,0:T(2,128)S(1)} %copy.18), channel_id=1, source_target_pairs={{0,1},{1,2},{2,3},{3,4},{4,5},{5,6},{6,7},{7,0},{8,9},{9,10},{10,1... | collective-permute-start | bytes 207368 | tf_op jit(solution)/shard_map/ppermute | solution.py:24
  142.8 6.3 %collective-permute-start.11 = (f32[3,80,36,2]{1,3,2,0:T(2,128)S(1)}, f32[3,80,36,2]{1,3,2,0:T(2,128)S(1)}, u32[]{:S(2)}, u32[]{:S(2)}) collective-permute-start(f32[3,80,36,2]{1,3,2,0:T(2,128)S(1)} %copy.19), channel_id=1, source_target_pairs={{1,0},{2,1},{3,2},{4,3},{5,4},{6,5},{7,6},{0,7},{9,8},{10,9},{11,1... | collective-permute-start | bytes 207368 | tf_op jit(solution)/shard_map/ppermute | solution.py:27
  163.3 2.3 copy-start.26
  165.7 5.7 %copy-start.6 = (f32[80,32,128]{2,1,0:T(8,128)S(1)}, f32[80,32,128]{2,1,0:T(8,128)}, u32[]{:S(2)}) copy-start(f32[80,32,128]{2,1,0:T(8,128)} %copy-done.5) | copy-start | bytes 3932164
  165.7 5.7 %copy-start.8 = (f32[80,32,128]{2,1,0:T(8,128)S(1)}, f32[80,32,128]{2,1,0:T(8,128)}, u32[]{:S(2)}) copy-start(f32[80,32,128]{2,1,0:T(8,128)} %copy-done.7) | copy-start | bytes 3932164
  172.8 1.2 copy-start
  173.1 0.9 copy-start.21
  173.1 0.9 copy-start.22
  173.1 0.9 copy-start.23
  174.0 1.9 copy-start.3
  175.8 7.7 %collective-permute-start.12 = (f32[80,32,128]{2,1,0:T(8,128)S(1)}, f32[80,32,128]{2,1,0:T(8,128)S(1)}, u32[]{:S(2)}, u32[]{:S(2)}) collective-permute-start(f32[80,32,128]{2,1,0:T(8,128)S(1)} %add_multiply_fusion.1), channel_id=1, source_target_pairs={{0,8},{8,16},{16,24},{24,32},{32,40},{40,48},{48,56},{56,64},{64,7... | collective-permute-start | bytes 3932168 | tf_op jit(solution)/shard_map/ppermute | solution.py:24
  181.0 5.6 %collective-permute-start.13 = (f32[80,32,128]{2,1,0:T(8,128)S(1)}, f32[80,32,128]{2,1,0:T(8,128)S(1)}, u32[]{:S(2)}, u32[]{:S(2)}) collective-permute-start(f32[80,32,128]{2,1,0:T(8,128)S(1)} %add_multiply_fusion.1), channel_id=1, source_target_pairs={{8,0},{16,8},{24,16},{32,24},{40,32},{48,40},{56,48},{64,56},{72,6... | collective-permute-start | bytes 3932168 | tf_op jit(solution)/shard_map/ppermute | solution.py:27
  189.0 1.1 copy-start.20
  194.0 30.6 %collective-permute-start.14 = (f32[80,32,32]{0,2,1:T(8,128)S(1)}, f32[80,32,32]{0,2,1:T(8,128)}, u32[]{:S(2)}, u32[]{:S(2)}) collective-permute-start(f32[80,32,32]{0,2,1:T(8,128)S(1)} %copy.22), channel_id=1, source_target_pairs={{0,1},{1,2},{2,3},{3,4},{4,5},{5,6},{6,7},{7,0},{8,9},{9,10},{10,1... | collective-permute-start | bytes 983048 | tf_op jit(solution)/shard_map/ppermute | solution.py:24
  198.2 29.4 %collective-permute-start.15 = (f32[80,32,32]{0,2,1:T(8,128)}, f32[80,32,32]{0,2,1:T(8,128)}, u32[]{:S(2)}, u32[]{:S(2)}) collective-permute-start(f32[80,32,32]{0,2,1:T(8,128)} %copy.23), channel_id=1, source_target_pairs={{1,0},{2,1},{3,2},{4,3},{5,4},{6,5},{7,6},{0,7},{9,8},{10,9},{11,1... | collective-permute-start | bytes 983048 | tf_op jit(solution)/shard_map/ppermute | solution.py:27
  230.6 30.2 %copy-start.27 = (s32[2]{0:T(128)S(1)}, s32[2]{0:T(128)}, u32[]{:S(2)}) copy-start(s32[2]{0:T(128)} %param.13) | copy-start | bytes 28
  285.7 1.7 copy-start.1
  287.4 2.1 copy-start.4
  290.0 3.9 collective-permute-start.16
  291.4 5.3 %collective-permute-start.17 = (f32[80,32,128]{2,1,0:T(8,128)S(1)}, f32[80,32,128]{2,1,0:T(8,128)S(1)}, u32[]{:S(2)}, u32[]{:S(2)}) collective-permute-start(f32[80,32,128]{2,1,0:T(8,128)S(1)} %add_multiply_fusion), channel_id=1, source_target_pairs={{8,0},{16,8},{24,16},{32,24},{40,32},{48,40},{56,48},{64,56},{72,6... | collective-permute-start | bytes 3932168 | tf_op jit(solution)/shard_map/ppermute | solution.py:27
  299.0 1.1 copy-start.19
  304.0 16.0 %collective-permute-start.18 = (f32[80,32,32]{0,2,1:T(8,128)S(1)}, f32[80,32,32]{0,2,1:T(8,128)}, u32[]{:S(2)}, u32[]{:S(2)}) collective-permute-start(f32[80,32,32]{0,2,1:T(8,128)S(1)} %copy.26), channel_id=1, source_target_pairs={{0,1},{1,2},{2,3},{3,4},{4,5},{5,6},{6,7},{7,0},{8,9},{9,10},{10,1... | collective-permute-start | bytes 983048 | tf_op jit(solution)/shard_map/ppermute | solution.py:24
  310.4 13.8 %collective-permute-start.19 = (f32[80,32,32]{0,2,1:T(8,128)}, f32[80,32,32]{0,2,1:T(8,128)}, u32[]{:S(2)}, u32[]{:S(2)}) collective-permute-start(f32[80,32,32]{0,2,1:T(8,128)} %copy.27), channel_id=1, source_target_pairs={{1,0},{2,1},{3,2},{4,3},{5,4},{6,5},{7,6},{0,7},{9,8},{10,9},{11,1... | collective-permute-start | bytes 983048 | tf_op jit(solution)/shard_map/ppermute | solution.py:27
  395.7 2.1 copy-start.2
where the time goes:
time: 406 us; the launch traced here: 401 us
  blocking collectives  107 us (26%)
  local copies, waits for them, and re-layouts  101 us (25%)
  other arithmetic  68.6 us (17%)
  starting transfers between devices  51.6 us (13%)
  waiting for transfers between devices  51.5 us (13%)
  matrix products  17.9 us (4%)
  between operations  4.12 us (1%)
    psum x10, blocking collectives, one_axis_at_a_time(): array = lax.psum(array, axis)  107 us
    concatenate x6, other arithmetic, extended(): block = jnp.concatenate([low, block, high], axis=dim)  36.1 us
    slice x10, local copies, waits for them, and re-layouts, extended(): lax.slice_in_dim(block, block.shape[dim] - width, None, axis=dim)  35.3 us
    ppermute x10, starting transfers between devices, extended(): lax.ppermute(lax.slice_in_dim(block, block.shape[dim] - width, None, axis...  33.7 us
    ppermute x10, waiting for transfers between devices, extended(): lax.ppermute(lax.slice_in_dim(block, block.shape[dim] - width, None, axis...  32.4 us
    ppermute x10, waiting for transfers between devices, extended(): lax.ppermute(lax.slice_in_dim(block, 0, width, axis=dim), axis, backward)  19.1 us
    ppermute x10, starting transfers between devices, extended(): lax.ppermute(lax.slice_in_dim(block, 0, width, axis=dim), axis, backward)  17.9 us
    select_n x3, other arithmetic, advance_deep(): jnp.where(valid_rows[None, :, None], wide_height, jnp.zeros_like(wide_hei...  17.3 us
  transfers between devices with their start and end apart: 20, of which 13 were waited for; matrix products, arithmetic and copies ran while one was open for 9% of the time, Pallas kernels for 0%

commit v1 on v0

--- a/solution.py
+++ b/solution.py
@@ -31,7 +31,8 @@
 
 def one_axis_at_a_time(array, axes):
     for axis in axes:
-        array = lax.psum(array, axis)
+        parts = lax.all_gather(array, axis)
+        array = jnp.sum(parts, axis=0)
     return array
 
 

time: 406 us -> 421 us (1.037)
  local copies, waits for them, and re-layouts: 101 us -> 118 us
  other arithmetic: 68.6 us -> 74.6 us
  blocking collectives: 107 us -> 101 us
    psum x10 -> x0, blocking collectives: 107 us -> none  [one_axis_at_a_time(): array = lax.psum(array, axis)]
    unnamed x0 -> x10, blocking collectives: none -> 101 us
    unnamed x56 -> x91, local copies, waits for them, and re-layouts: 5.32 us -> 22.1 us
    reduce_sum x0 -> x10, other arithmetic: none -> 6.03 us  [one_axis_at_a_time(): array = jnp.sum(parts, axis=0)]
where the time goes in v1:
time: 421 us; the launch traced here: 416 us
  local copies, waits for them, and re-layouts  118 us (28%)
  blocking collectives  101 us (24%)
  other arithmetic  74.6 us (18%)
  starting transfers between devices  51.4 us (12%)
  waiting for transfers between devices  49.8 us (12%)
  matrix products  18 us (4%)
    unnamed x10, blocking collectives  101 us
    concatenate x6, other arithmetic, extended(): block = jnp.concatenate([low, block, high], axis=dim)  36.1 us
    slice x10, local copies, waits for them, and re-layouts, extended(): lax.slice_in_dim(block, block.shape[dim] - width, None, axis=dim)  35.5 us
    ppermute x10, starting transfers between devices, extended(): lax.ppermute(lax.slice_in_dim(block, block.shape[dim] - width, None, axis...  33.7 us
    ppermute x10, waiting for transfers between devices, extended(): lax.ppermute(lax.slice_in_dim(block, block.shape[dim] - width, None, axis...  30.6 us
    unnamed x91, local copies, waits for them, and re-layouts  22.1 us
    ppermute x10, waiting for transfers between devices, extended(): lax.ppermute(lax.slice_in_dim(block, 0, width, axis=dim), axis, backward)  19.1 us
    ppermute x10, starting transfers between devices, extended(): lax.ppermute(lax.slice_in_dim(block, 0, width, axis=dim), axis, backward)  17.7 us
  transfers between devices with their start and end apart: 20, of which 13 were waited for; matrix products, arithmetic and copies ran while one was open for 9% of the time, Pallas kernels for 0%

profile of v1, /device:TPU:2, one launch (start us, length us, event | category | flops | bytes accessed | tf_op | source)
XLA Modules:
  0.0 416.2 jit_solution(14252123621898880435)
XLA Ops:
  0.7 2.5 pad_maximum_fusion.15
  6.2 3.4 collective-permute-done.1
  9.7 2.1 pad_maximum_fusion.3
  11.8 5.3 %fusion.117 = (f32[3,80,36,2]{3,2,1,0:T(8,128)}, f32[3,80,36,2]{3,2,1,0:T(8,128)}) fusion(f32[3,80,36,128]{3,2,1,0:T(8,128)S(1)} %pad_maximum_fusion.3), kind=kLoop, calls=%fused_computation.180 | loop fusion | bytes 276480 | tf_op jit(solution)/shard_map/slice | solution.py:25
  17.1 3.8 copy.10
  20.9 3.9 collective-permute-start.2
  24.9 3.8 copy.11
  30.3 3.6 copy.12
  35.5 3.5 copy.13
  39.0 10.7 %pad_maximum_fusion = f32[3,80,36,132]{3,2,1,0:T(8,128)S(1)} fusion(f32[3,80,36,2]{3,2,1,0:T(8,128)} %copy.13, f32[3,80,2,128]{3,2,1,0:T(2,128)S(1)} %collective-permute-done.1, f32[1,80,32,128]{3,2,1,0:T(8,128)S(1)} %bitcast.140, f32[1,80,32,128]{3,2,1,0:T(8,128)S(1)} %bitcast.143, f32[1,80,32,128]{3,2,1,0:T(8,128)} %bitcast.146, ...), kind=kLoop, calls=%fused_computation | loop fusion | flops 6842880 | bytes 9123840 | tf_op jit(solution)/shard_map/concatenate | solution.py:28
  49.7 2.3 slice_bitcast_fusion.8
  52.0 5.8 %fusion.23 = f32[80,34,130]{2,1,0:T(8,128)S(1)} fusion(f32[80,36,132]{2,1,0:T(8,128)S(1)} %get-tuple-element.10, f32[80,36,132]{2,1,0:T(8,128)S(1)} %get-tuple-element.11, f32[80,36,132]{2,1,0:T(8,128)} %get-tuple-element.9, pred[34]{0:T(512)(128)(4,1)S(1)} %copy-done.24), kind=kLoop, calls=%fused_computation.44 | loop fusion | flops 2121600 | bytes 8486434 | tf_op jit(solution)/shard_map/jit(_where)/select_n | solution.py:76
  59.5 5.1 %collective-permute-start.4 = (f32[3,80,2,128]{3,2,1,0:T(2,128)S(1)}, f32[3,80,2,128]{3,2,1,0:T(2,128)S(1)}, u32[]{:S(2)}, u32[]{:S(2)}) collective-permute-start(f32[3,80,2,128]{3,2,1,0:T(2,128)S(1)} %get-tuple-element.29), channel_id=1, source_target_pairs={{0,8},{8,16},{16,24},{24,32},{32,40},{40,48},{48,56},{56,64},{64,7... | collective-permute-start | bytes 737288 | tf_op jit(solution)/shard_map/ppermute | solution.py:24
  66.1 3.3 collective-permute-done.5
  70.4 5.3 %fusion.116 = (f32[3,80,36,2]{3,2,1,0:T(8,128)}, f32[3,80,36,2]{3,2,1,0:T(8,128)}) fusion(f32[3,80,36,128]{3,2,1,0:T(8,128)S(1)} %pad_maximum_fusion.4), kind=kLoop, calls=%fused_computation.179 | loop fusion | bytes 276480 | tf_op jit(solution)/shard_map/slice | solution.py:25
  75.7 3.8 copy.14
  81.1 3.8 copy.15
  85.0 3.0 collective-permute-start.7
  88.0 3.6 copy.16
  91.6 3.5 copy.17
  95.1 10.7 %pad_maximum_fusion.1 = f32[3,80,36,132]{3,2,1,0:T(8,128)S(1)} fusion(f32[3,80,36,2]{3,2,1,0:T(8,128)} %copy.17, f32[3,80,2,128]{3,2,1,0:T(2,128)S(1)} %collective-permute-done.5, f32[1,80,32,128]{3,2,1,0:T(8,128)S(1)} %bitcast.137, f32[1,80,32,128]{3,2,1,0:T(8,128)S(1)} %bitcast.134, f32[1,80,32,128]{3,2,1,0:T(8,128)} %copy-done.18, ...), kind=kLoop, calls=%fused_computation.1 | loop fusion | flops 6842880 | bytes 9123840 | tf_op jit(solution)/shard_map/concatenate | solution.py:28
  105.8 2.3 slice_bitcast_fusion.5
  108.1 5.8 %fusion.19 = f32[80,34,130]{2,1,0:T(8,128)S(1)} fusion(f32[80,36,132]{2,1,0:T(8,128)S(1)} %get-tuple-element.7, f32[80,36,132]{2,1,0:T(8,128)S(1)} %get-tuple-element.8, f32[80,36,132]{2,1,0:T(8,128)} %get-tuple-element.6, pred[34]{0:T(512)(128)(4,1)S(1)} %copy-done.25), kind=kLoop, calls=%fused_computation.35 | loop fusion | flops 2121600 | bytes 8486434 | tf_op jit(solution)/shard_map/jit(_where)/select_n | solution.py:76
  115.7 5.9 %collective-permute-start.8 = (f32[3,80,2,128]{3,2,1,0:T(2,128)S(1)}, f32[3,80,2,128]{3,2,1,0:T(2,128)S(1)}, u32[]{:S(2)}, u32[]{:S(2)}) collective-permute-start(f32[3,80,2,128]{3,2,1,0:T(2,128)S(1)} %get-tuple-element.27), channel_id=1, source_target_pairs={{0,8},{8,16},{16,24},{24,32},{32,40},{40,48},{48,56},{56,64},{64,7... | collective-permute-start | bytes 737288 | tf_op jit(solution)/shard_map/ppermute | solution.py:24
  125.9 5.3 %fusion.115 = (f32[3,80,36,2]{3,2,1,0:T(8,128)}, f32[3,80,36,2]{3,2,1,0:T(8,128)}) fusion(f32[3,80,36,128]{3,2,1,0:T(8,128)S(1)} %pad_maximum_fusion.5), kind=kLoop, calls=%fused_computation.178 | loop fusion | bytes 276480 | tf_op jit(solution)/shard_map/slice | solution.py:25
  131.3 3.8 copy.18
  135.1 3.9 collective-permute-start.10
  139.0 3.8 copy.19
  143.5 3.6 copy.20
  147.1 2.1 collective-permute-done.11
  149.2 3.5 copy.21
  152.7 10.7 %pad_maximum_fusion.2 = f32[3,80,36,132]{3,2,1,0:T(8,128)S(1)} fusion(f32[3,80,36,2]{3,2,1,0:T(8,128)} %copy.21, f32[3,80,2,128]{3,2,1,0:T(2,128)S(1)} %collective-permute-done.9, f32[1,80,32,128]{3,2,1,0:T(8,128)S(1)} %bitcast.131, f32[1,80,32,128]{3,2,1,0:T(8,128)S(1)} %bitcast.128, f32[1,80,32,128]{3,2,1,0:T(8,128)} %copy-done.17, ...), kind=kLoop, calls=%fused_computation.2 | loop fusion | flops 6842880 | bytes 9123840 | tf_op jit(solution)/shard_map/concatenate | solution.py:28
  163.4 2.3 slice_bitcast_fusion.2
  165.7 5.6 %fusion.15 = f32[80,34,130]{2,1,0:T(8,128)S(1)} fusion(f32[80,36,132]{2,1,0:T(8,128)S(1)} %get-tuple-element.4, f32[80,36,132]{2,1,0:T(8,128)S(1)} %get-tuple-element.5, f32[80,36,132]{2,1,0:T(8,128)} %get-tuple-element.3, pred[34]{0:T(512)(128)(4,1)S(1)} %copy-done.26), kind=kLoop, calls=%fused_computation.26 | loop fusion | flops 2121600 | bytes 8486434 | tf_op jit(solution)/shard_map/jit(_where)/select_n | solution.py:76
  175.9 5.2 %collective-permute-start.12 = (f32[80,32,128]{2,1,0:T(8,128)S(1)}, f32[80,32,128]{2,1,0:T(8,128)S(1)}, u32[]{:S(2)}, u32[]{:S(2)}) collective-permute-start(f32[80,32,128]{2,1,0:T(8,128)S(1)} %add_multiply_fusion.1), channel_id=1, source_target_pairs={{0,8},{8,16},{16,24},{24,32},{32,40},{40,48},{48,56},{56,64},{64,7... | collective-permute-start | bytes 3932168 | tf_op jit(solution)/shard_map/ppermute | solution.py:24
  183.6 3.1 collective-permute-done.13
  186.7 2.3 fusion.39
  192.0 2.0 copy.22
  195.5 2.8 copy.23
  198.3 3.0 collective-permute-start.15
  203.2 21.4 %collective-permute-done.14 = f32[80,32,32]{0,2,1:T(8,128)} collective-permute-done((f32[80,32,32]{0,2,1:T(8,128)S(1)}, f32[80,32,32]{0,2,1:T(8,128)}, u32[]{:S(2)}, u32[]{:S(2)}) %collective-permute-start.14) | collective-permute-done | bytes 327712 | tf_op jit(solution)/shard_map/ppermute | solution.py:24
  224.5 3.0 copy.24
  227.6 3.0 copy.25
  230.6 6.5 %multiply_reduce_fusion.3 = (f32[]{:T(128)}, f32[80,32,128]{2,1,0:T(8,128)}) fusion(s32[192]{0:T(256)S(1)} %iota_add_fusion, f32[80,32,32]{2,1,0:T(8,128)} %copy.25, f32[80,32,128]{2,1,0:T(8,128)} %copy-done.19, f32[80,32,32]{2,1,0:T(8,128)} %copy.24), kind=kOutput, calls=%fused_computation.99 | convolution fusion | flops 757137408 | bytes 3277572 | tf_op jit(solution)/shard_map/mrjk,bk->mrjb/dot_general | solution.py:57
  239.0 13.9 %all-reduce = f32[2]{0:T(128)S(1)} all-reduce(f32[2]{0:T(128)S(1)} %dynamic-update-slice), channel_id=1, replica_groups=mesh['member_0'=2,'member_1'=4,'member_2'=2,'band_0'=4,'band_1'=2] {'mem..., use_global_device_ids=true, to_apply=%add | all-reduce | flops 2 | bytes 16
  255.6 8.7 %all-reduce.1 = f32[4]{0:T(128)S(1)} all-reduce(f32[4]{0:T(128)S(1)} %dynamic-update-slice.1), channel_id=1, replica_groups=mesh['member_0'=2,'member_1'=4,'member_2'=2,'band_0'=4,'band_1'=2] {'mem..., use_global_device_ids=true, to_apply=%add.1 | all-reduce | flops 4 | bytes 32
  266.8 4.3 %all-reduce.2 = f32[2]{0:T(128)S(1)} all-reduce(f32[2]{0:T(128)S(1)} %dynamic-update-slice.2), channel_id=1, replica_groups=mesh['member_0'=2,'member_1'=4,'member_2'=2,'band_0'=4,'band_1'=2] {'mem..., use_global_device_ids=true, to_apply=%add.2 | all-reduce | flops 2 | bytes 16
  273.7 10.1 %all-reduce.3 = f32[4]{0:T(128)S(1)} all-reduce(f32[4]{0:T(128)S(1)} %dynamic-update-slice.3), channel_id=1, replica_groups=mesh['member_0'=2,'member_1'=4,'member_2'=2,'band_0'=4,'band_1'=2] {'ban..., use_global_device_ids=true, to_apply=%add.3 | all-reduce | flops 4 | bytes 32
  285.8 6.7 %all-reduce.4 = f32[2]{0:T(128)S(1)} all-reduce(f32[2]{0:T(128)S(1)} %dynamic-update-slice.4), channel_id=1, replica_groups=mesh['member_0'=2,'member_1'=4,'member_2'=2,'band_0'=4,'band_1'=2] {'ban..., use_global_device_ids=true, to_apply=%add.4 | all-reduce | flops 2 | bytes 16
  302.1 2.7 collective-permute-done.17
  304.8 2.3 fusion.36
  312.1 3.6 collective-permute-start.18
  315.7 2.8 copy.27
  318.5 2.7 collective-permute-start.19
  321.2 6.9 %collective-permute-done.18 = f32[80,32,32]{0,2,1:T(8,128)} collective-permute-done((f32[80,32,32]{0,2,1:T(8,128)S(1)}, f32[80,32,32]{0,2,1:T(8,128)}, u32[]{:S(2)}, u32[]{:S(2)}) %collective-permute-start.18) | collective-permute-done | bytes 327712 | tf_op jit(solution)/shard_map/ppermute | solution.py:24
  328.1 3.0 copy.28
  332.3 3.0 copy.29
  335.3 6.8 %multiply_reduce_fusion.2 = (f32[]{:T(128)}, f32[80,32,128]{2,1,0:T(8,128)}) fusion(s32[192]{0:T(256)S(1)} %iota_add_fusion, f32[80,32,32]{2,1,0:T(8,128)} %copy.29, f32[80,32,128]{2,1,0:T(8,128)} %copy-done.20, f32[80,32,32]{2,1,0:T(8,128)} %copy.28, f32[80,32,128]{2,1,0:T(8,128)} %get-tuple-element.47, f32[]{:T(128)S(6)} %div.55), kind=kOutput, calls=%fused_computation.96 | convolution fusion | flops 757792768 | bytes 4588296 | tf_op jit(solution)/shard_map/mrjk,bk->mrjb/dot_general | solution.py:57
  343.5 28.3 %all-reduce.5 = f32[2]{0:T(128)S(1)} all-reduce(f32[2]{0:T(128)S(1)} %dynamic-update-slice.5), channel_id=1, replica_groups=mesh['member_0'=2,'member_1'=4,'member_2'=2,'band_0'=4,'band_1'=2] {'mem..., use_global_device_ids=true, to_apply=%add.5 | all-reduce | flops 2 | bytes 16
  373.8 8.7 %all-reduce.6 = f32[4]{0:T(128)S(1)} all-reduce(f32[4]{0:T(128)S(1)} %dynamic-update-slice.6), channel_id=1, replica_groups=mesh['member_0'=2,'member_1'=4,'member_2'=2,'band_0'=4,'band_1'=2] {'mem..., use_global_device_ids=true, to_apply=%add.6 | all-reduce | flops 4 | bytes 32
  384.5 2.4 all-reduce.7
  389.6 10.7 %all-reduce.8 = f32[4]{0:T(128)S(1)} all-reduce(f32[4]{0:T(128)S(1)} %dynamic-update-slice.8), channel_id=1, replica_groups=mesh['member_0'=2,'member_1'=4,'member_2'=2,'band_0'=4,'band_1'=2] {'ban..., use_global_device_ids=true, to_apply=%add.8 | all-reduce | flops 4 | bytes 32
  402.3 7.0 %all-reduce.9 = f32[2]{0:T(128)S(1)} all-reduce(f32[2]{0:T(128)S(1)} %dynamic-update-slice.9), channel_id=1, replica_groups=mesh['member_0'=2,'member_1'=4,'member_2'=2,'band_0'=4,'band_1'=2] {'ban..., use_global_device_ids=true, to_apply=%add.9 | all-reduce | flops 2 | bytes 16
  410.5 2.1 subtract_multiply_fusion.1
  (154 shorter events, 70.9 us)
Async XLA Ops:
  0.6 9.0 %copy-start.15 = (f32[80,32,128]{2,1,0:T(8,128)S(1)}, f32[80,32,128]{2,1,0:T(8,128)}, u32[]{:S(2)}) copy-start(f32[80,32,128]{2,1,0:T(8,128)} %param.8) | copy-start | bytes 3932164
  0.6 9.0 %copy-start.13 = (f32[80,32,128]{2,1,0:T(8,128)S(1)}, f32[80,32,128]{2,1,0:T(8,128)}, u32[]{:S(2)}) copy-start(f32[80,32,128]{2,1,0:T(8,128)} %param.9) | copy-start | bytes 3932164
  3.2 3.1 collective-permute-start
  4.9 4.8 %collective-permute-start.1 = (f32[3,80,2,128]{3,2,1,0:T(2,128)S(1)}, f32[3,80,2,128]{3,2,1,0:T(2,128)S(1)}, u32[]{:S(2)}, u32[]{:S(2)}) collective-permute-start(f32[3,80,2,128]{3,2,1,0:T(2,128)S(1)} %get-tuple-element.32), channel_id=1, source_target_pairs={{8,0},{16,8},{24,16},{32,24},{40,32},{48,40},{56,48},{64,56},{72,6... | collective-permute-start | bytes 737288 | tf_op jit(solution)/shard_map/ppermute | solution.py:27
  20.9 9.4 %collective-permute-start.2 = (f32[3,80,36,2]{1,3,2,0:T(2,128)S(1)}, f32[3,80,36,2]{1,3,2,0:T(2,128)S(1)}, u32[]{:S(2)}, u32[]{:S(2)}) collective-permute-start(f32[3,80,36,2]{1,3,2,0:T(2,128)S(1)} %copy.10), channel_id=1, source_target_pairs={{0,1},{1,2},{2,3},{3,4},{4,5},{5,6},{6,7},{7,0},{8,9},{9,10},{10,1... | collective-permute-start | bytes 207368 | tf_op jit(solution)/shard_map/ppermute | solution.py:24
  28.7 6.8 %collective-permute-start.3 = (f32[3,80,36,2]{1,3,2,0:T(2,128)S(1)}, f32[3,80,36,2]{1,3,2,0:T(2,128)S(1)}, u32[]{:S(2)}, u32[]{:S(2)}) collective-permute-start(f32[3,80,36,2]{1,3,2,0:T(2,128)S(1)} %copy.11), channel_id=1, source_target_pairs={{1,0},{2,1},{3,2},{4,3},{5,4},{6,5},{7,6},{0,7},{9,8},{10,9},{11,1... | collective-permute-start | bytes 207368 | tf_op jit(solution)/shard_map/ppermute | solution.py:27
  49.7 2.3 copy-start.24
  52.0 5.9 %copy-start.14 = (f32[80,32,128]{2,1,0:T(8,128)S(1)}, f32[80,32,128]{2,1,0:T(8,128)}, u32[]{:S(2)}) copy-start(f32[80,32,128]{2,1,0:T(8,128)} %param.9) | copy-start | bytes 3932164
  52.0 5.9 %copy-start.16 = (f32[80,32,128]{2,1,0:T(8,128)S(1)}, f32[80,32,128]{2,1,0:T(8,128)}, u32[]{:S(2)}) copy-start(f32[80,32,128]{2,1,0:T(8,128)} %param.8) | copy-start | bytes 3932164
  59.3 16.4 %copy-start.18 = (f32[1,80,32,128]{3,2,1,0:T(8,128)}, f32[1,80,32,128]{3,2,1,0:T(8,128)S(1)}, u32[]{:S(2)}) copy-start(f32[1,80,32,128]{3,2,1,0:T(8,128)S(1)} %get-tuple-element.35) | copy-start | bytes 3932164
  59.3 35.8 %copy-start.9 = (f32[80,32,128]{2,1,0:T(8,128)}, f32[80,32,128]{2,1,0:T(8,128)S(1)}, u32[]{:S(2)}) copy-start(f32[80,32,128]{2,1,0:T(8,128)S(1)} %get-tuple-element.16) | copy-start | bytes 3932164
  59.3 35.7 %copy-start.11 = (f32[80,32,128]{2,1,0:T(8,128)}, f32[80,32,128]{2,1,0:T(8,128)S(1)}, u32[]{:S(2)}) copy-start(f32[80,32,128]{2,1,0:T(8,128)S(1)} %get-tuple-element.17) | copy-start | bytes 3932164
  59.5 6.6 %collective-permute-start.4 = (f32[3,80,2,128]{3,2,1,0:T(2,128)S(1)}, f32[3,80,2,128]{3,2,1,0:T(2,128)S(1)}, u32[]{:S(2)}, u32[]{:S(2)}) collective-permute-start(f32[3,80,2,128]{3,2,1,0:T(2,128)S(1)} %get-tuple-element.29), channel_id=1, source_target_pairs={{0,8},{8,16},{16,24},{24,32},{32,40},{40,48},{48,56},{56,64},{64,7... | collective-permute-start | bytes 737288 | tf_op jit(solution)/shard_map/ppermute | solution.py:24
  64.6 4.8 %collective-permute-start.5 = (f32[3,80,2,128]{3,2,1,0:T(2,128)S(1)}, f32[3,80,2,128]{3,2,1,0:T(2,128)S(1)}, u32[]{:S(2)}, u32[]{:S(2)}) collective-permute-start(f32[3,80,2,128]{3,2,1,0:T(2,128)S(1)} %get-tuple-element.30), channel_id=1, source_target_pairs={{8,0},{16,8},{24,16},{32,24},{40,32},{48,40},{56,48},{64,56},{72,6... | collective-permute-start | bytes 737288 | tf_op jit(solution)/shard_map/ppermute | solution.py:27
  79.6 8.4 %collective-permute-start.6 = (f32[3,80,36,2]{1,3,2,0:T(2,128)S(1)}, f32[3,80,36,2]{1,3,2,0:T(2,128)S(1)}, u32[]{:S(2)}, u32[]{:S(2)}) collective-permute-start(f32[3,80,36,2]{1,3,2,0:T(2,128)S(1)} %copy.14), channel_id=1, source_target_pairs={{0,1},{1,2},{2,3},{3,4},{4,5},{5,6},{6,7},{7,0},{8,9},{9,10},{10,1... | collective-permute-start | bytes 207368 | tf_op jit(solution)/shard_map/ppermute | solution.py:24
  85.0 6.7 %collective-permute-start.7 = (f32[3,80,36,2]{1,3,2,0:T(2,128)S(1)}, f32[3,80,36,2]{1,3,2,0:T(2,128)S(1)}, u32[]{:S(2)}, u32[]{:S(2)}) collective-permute-start(f32[3,80,36,2]{1,3,2,0:T(2,128)S(1)} %copy.15), channel_id=1, source_target_pairs={{1,0},{2,1},{3,2},{4,3},{5,4},{6,5},{7,6},{0,7},{9,8},{10,9},{11,1... | collective-permute-start | bytes 207368 | tf_op jit(solution)/shard_map/ppermute | solution.py:27
  105.8 2.3 copy-start.25
  108.1 5.9 %copy-start.10 = (f32[80,32,128]{2,1,0:T(8,128)S(1)}, f32[80,32,128]{2,1,0:T(8,128)}, u32[]{:S(2)}) copy-start(f32[80,32,128]{2,1,0:T(8,128)} %copy-done.9) | copy-start | bytes 3932164
  108.1 5.9 %copy-start.12 = (f32[80,32,128]{2,1,0:T(8,128)S(1)}, f32[80,32,128]{2,1,0:T(8,128)}, u32[]{:S(2)}) copy-start(f32[80,32,128]{2,1,0:T(8,128)} %copy-done.11) | copy-start | bytes 3932164
  115.4 15.8 %copy-start.17 = (f32[1,80,32,128]{3,2,1,0:T(8,128)}, f32[1,80,32,128]{3,2,1,0:T(8,128)S(1)}, u32[]{:S(2)}) copy-start(f32[1,80,32,128]{3,2,1,0:T(8,128)S(1)} %get-tuple-element.34) | copy-start | bytes 3932164
  115.4 37.2 %copy-start.5 = (f32[80,32,128]{2,1,0:T(8,128)}, f32[80,32,128]{2,1,0:T(8,128)S(1)}, u32[]{:S(2)}) copy-start(f32[80,32,128]{2,1,0:T(8,128)S(1)} %get-tuple-element.14) | copy-start | bytes 3932164
  115.4 37.2 %copy-start.7 = (f32[80,32,128]{2,1,0:T(8,128)}, f32[80,32,128]{2,1,0:T(8,128)S(1)}, u32[]{:S(2)}) copy-start(f32[80,32,128]{2,1,0:T(8,128)S(1)} %get-tuple-element.15) | copy-start | bytes 3932164
  115.7 7.6 %collective-permute-start.8 = (f32[3,80,2,128]{3,2,1,0:T(2,128)S(1)}, f32[3,80,2,128]{3,2,1,0:T(2,128)S(1)}, u32[]{:S(2)}, u32[]{:S(2)}) collective-permute-start(f32[3,80,2,128]{3,2,1,0:T(2,128)S(1)} %get-tuple-element.27), channel_id=1, source_target_pairs={{0,8},{8,16},{16,24},{24,32},{32,40},{40,48},{48,56},{56,64},{64,7... | collective-permute-start | bytes 737288 | tf_op jit(solution)/shard_map/ppermute | solution.py:24
  121.6 3.4 collective-permute-start.9
  135.1 8.4 %collective-permute-start.10 = (f32[3,80,36,2]{1,3,2,0:T(2,128)S(1)}, f32[3,80,36,2]{1,3,2,0:T(2,128)S(1)}, u32[]{:S(2)}, u32[]{:S(2)}) collective-permute-start(f32[3,80,36,2]{1,3,2,0:T(2,128)S(1)} %copy.18), channel_id=1, source_target_pairs={{0,1},{1,2},{2,3},{3,4},{4,5},{5,6},{6,7},{7,0},{8,9},{9,10},{10,1... | collective-permute-start | bytes 207368 | tf_op jit(solution)/shard_map/ppermute | solution.py:24
  142.9 6.3 %collective-permute-start.11 = (f32[3,80,36,2]{1,3,2,0:T(2,128)S(1)}, f32[3,80,36,2]{1,3,2,0:T(2,128)S(1)}, u32[]{:S(2)}, u32[]{:S(2)}) collective-permute-start(f32[3,80,36,2]{1,3,2,0:T(2,128)S(1)} %copy.19), channel_id=1, source_target_pairs={{1,0},{2,1},{3,2},{4,3},{5,4},{6,5},{7,6},{0,7},{9,8},{10,9},{11,1... | collective-permute-start | bytes 207368 | tf_op jit(solution)/shard_map/ppermute | solution.py:27
  163.4 2.3 copy-start.26
  165.7 5.7 %copy-start.6 = (f32[80,32,128]{2,1,0:T(8,128)S(1)}, f32[80,32,128]{2,1,0:T(8,128)}, u32[]{:S(2)}) copy-start(f32[80,32,128]{2,1,0:T(8,128)} %copy-done.5) | copy-start | bytes 3932164
  165.7 5.7 %copy-start.8 = (f32[80,32,128]{2,1,0:T(8,128)S(1)}, f32[80,32,128]{2,1,0:T(8,128)}, u32[]{:S(2)}) copy-start(f32[80,32,128]{2,1,0:T(8,128)} %copy-done.7) | copy-start | bytes 3932164
  172.8 1.2 copy-start
  173.1 0.9 copy-start.21
  173.1 0.9 copy-start.22
  173.2 0.9 copy-start.23
  174.0 1.9 copy-start.3
  175.9 7.7 %collective-permute-start.12 = (f32[80,32,128]{2,1,0:T(8,128)S(1)}, f32[80,32,128]{2,1,0:T(8,128)S(1)}, u32[]{:S(2)}, u32[]{:S(2)}) collective-permute-start(f32[80,32,128]{2,1,0:T(8,128)S(1)} %add_multiply_fusion.1), channel_id=1, source_target_pairs={{0,8},{8,16},{16,24},{24,32},{32,40},{40,48},{48,56},{56,64},{64,7... | collective-permute-start | bytes 3932168 | tf_op jit(solution)/shard_map/ppermute | solution.py:24
  181.0 5.6 %collective-permute-start.13 = (f32[80,32,128]{2,1,0:T(8,128)S(1)}, f32[80,32,128]{2,1,0:T(8,128)S(1)}, u32[]{:S(2)}, u32[]{:S(2)}) collective-permute-start(f32[80,32,128]{2,1,0:T(8,128)S(1)} %add_multiply_fusion.1), channel_id=1, source_target_pairs={{8,0},{16,8},{24,16},{32,24},{40,32},{48,40},{56,48},{64,56},{72,6... | collective-permute-start | bytes 3932168 | tf_op jit(solution)/shard_map/ppermute | solution.py:27
  189.0 1.1 copy-start.19
  192.0 9.3 %copy-start.32 = (u32[128]{0:T(128)S(1)}, u32[128]{0:T(128)}, u32[]{:S(2)}) copy-start(u32[128]{0:T(128)} %constant.81) | copy-start | bytes 1540
  192.0 9.9 %copy-start.31 = (u32[128]{0:T(128)S(1)}, u32[128]{0:T(128)}, u32[]{:S(2)}) copy-start(u32[128]{0:T(128)} %constant.86) | copy-start | bytes 1540
  192.0 10.5 %copy-start.27 = (s32[2]{0:T(128)S(1)}, s32[2]{0:T(128)}, u32[]{:S(2)}) copy-start(s32[2]{0:T(128)} %param.13) | copy-start | bytes 28
  194.1 30.5 %collective-permute-start.14 = (f32[80,32,32]{0,2,1:T(8,128)S(1)}, f32[80,32,32]{0,2,1:T(8,128)}, u32[]{:S(2)}, u32[]{:S(2)}) collective-permute-start(f32[80,32,32]{0,2,1:T(8,128)S(1)} %copy.22), channel_id=1, source_target_pairs={{0,1},{1,2},{2,3},{3,4},{4,5},{5,6},{6,7},{7,0},{8,9},{9,10},{10,1... | collective-permute-start | bytes 983048 | tf_op jit(solution)/shard_map/ppermute | solution.py:24
  198.3 29.3 %collective-permute-start.15 = (f32[80,32,32]{0,2,1:T(8,128)}, f32[80,32,32]{0,2,1:T(8,128)}, u32[]{:S(2)}, u32[]{:S(2)}) collective-permute-start(f32[80,32,32]{0,2,1:T(8,128)} %copy.23), channel_id=1, source_target_pairs={{1,0},{2,1},{3,2},{4,3},{5,4},{6,5},{7,6},{0,7},{9,8},{10,9},{11,1... | collective-permute-start | bytes 983048 | tf_op jit(solution)/shard_map/ppermute | solution.py:27
  230.6 7.8 %copy-start.30 = (u32[128]{0:T(128)S(1)}, u32[128]{0:T(128)}, u32[]{:S(2)}) copy-start(u32[128]{0:T(128)} %constant.91) | copy-start | bytes 1540
  230.6 24.3 %copy-start.29 = (u32[128]{0:T(128)S(1)}, u32[128]{0:T(128)}, u32[]{:S(2)}) copy-start(u32[128]{0:T(128)} %constant.96) | copy-start | bytes 1540
  230.6 35.6 %copy-start.28 = (u32[128]{0:T(128)S(1)}, u32[128]{0:T(128)}, u32[]{:S(2)}) copy-start(u32[128]{0:T(128)} %constant.101) | copy-start | bytes 1540
  293.8 1.7 copy-start.1
  295.5 2.1 copy-start.4
  298.1 3.9 collective-permute-start.16
  299.5 5.3 %collective-permute-start.17 = (f32[80,32,128]{2,1,0:T(8,128)S(1)}, f32[80,32,128]{2,1,0:T(8,128)S(1)}, u32[]{:S(2)}, u32[]{:S(2)}) collective-permute-start(f32[80,32,128]{2,1,0:T(8,128)S(1)} %add_multiply_fusion), channel_id=1, source_target_pairs={{8,0},{16,8},{24,16},{32,24},{40,32},{48,40},{56,48},{64,56},{72,6... | collective-permute-start | bytes 3932168 | tf_op jit(solution)/shard_map/ppermute | solution.py:27
  307.2 1.1 copy-start.20
  312.1 16.0 %collective-permute-start.18 = (f32[80,32,32]{0,2,1:T(8,128)S(1)}, f32[80,32,32]{0,2,1:T(8,128)}, u32[]{:S(2)}, u32[]{:S(2)}) collective-permute-start(f32[80,32,32]{0,2,1:T(8,128)S(1)} %copy.26), channel_id=1, source_target_pairs={{0,1},{1,2},{2,3},{3,4},{4,5},{5,6},{6,7},{7,0},{8,9},{9,10},{10,1... | collective-permute-start | bytes 983048 | tf_op jit(solution)/shard_map/ppermute | solution.py:24
  318.5 13.8 %collective-permute-start.19 = (f32[80,32,32]{0,2,1:T(8,128)}, f32[80,32,32]{0,2,1:T(8,128)}, u32[]{:S(2)}, u32[]{:S(2)}) collective-permute-start(f32[80,32,32]{0,2,1:T(8,128)} %copy.27), channel_id=1, source_target_pairs={{1,0},{2,1},{3,2},{4,3},{5,4},{6,5},{7,6},{0,7},{9,8},{10,9},{11,1... | collective-permute-start | bytes 983048 | tf_op jit(solution)/shard_map/ppermute | solution.py:27
  410.5 2.1 copy-start.2
